TPU v7x, 128 devices: a whole 4x4x4 slice. The times are simulated.
128 devices in a mesh: table: 8 (over y, core), ray: 16 (over x, z).
Axes of the slice: x: 4, y: 4, z: 4, core: 2. Of those that a mesh axis runs over, the one named last changes fastest.
Arguments:
- table: float32 [2, 8192, 4, 512], P(None, ('table', 'ray')), may hold values from -6 to 6
- moment1: float32 [2, 8192, 4, 512], P(None, ('table', 'ray')), may hold values from -2 to 2
- moment2: float32 [2, 8192, 4, 512], P(None, ('table', 'ray')), may hold values from 0.01 to 1
- block_ids: int32 [8, 2, 128, 4], replicated, may hold values from 0 to 63, as said below
- sample_slot: int32 [2, 65536], P(None, ('table', 'ray')), may hold values from 0 to 511, as said below
- corners: int32 [2, 8, 65536], P(None, None, ('table', 'ray')), may hold values from 0 to 511
- fractions: float32 [2, 3, 65536], P(None, None, ('table', 'ray')), may hold values from 0 to 1
- feat_cot: float32 [2, 4, 65536], P(None, None, ('table', 'ray')), may hold values from -24 to 24
- weight_in: float32 [64, 8], replicated, may hold values from -2 to 2
- weight_out: float32 [16, 64], replicated, may hold values from -0.75 to 0.75
Outputs:
- table_new: float32 [2, 8192, 4, 512], P(None, ('table', 'ray'))
- moment1_new: float32 [2, 8192, 4, 512], P(None, ('table', 'ray'))
- moment2_new: float32 [2, 8192, 4, 512], P(None, ('table', 'ray'))
- mlp_out: float32 [16, 65536], P(None, ('table', 'ray'))
Inputs may be any that keep to these rules, and one draw needn't show every extreme that they name: `block_ids`: for every group, level and owner the 4 listed blocks are distinct local block numbers of that owner. `sample_slot`: each device's 512 samples of a level come in 16 runs of 512 // 16 in order; the samples of run i read only blocks of owners o with o % 16 == i.
All inputs are finite; a program needn't handle non-finite values.
Results may differ from a plain program's by a relative error of at most 0.000075.
Values sent between devices are 32-bit elements; how exact they have to be, the bound alone decides.
No kernel may reach another device: no remote copies, remote signals or barrier semaphores. Data moves between devices by JAX's collectives and lax.ppermute only.
A program may use at most 64 MiB of HBM per device.

v0:
```python
import jax
import jax.numpy as jnp
from jax import lax
from jax.sharding import PartitionSpec as P

beta_one = 0.9
beta_two = 0.99
learn_rate = 0.01
adam_eps = 1e-15


def hat_weights(fractions):
    columns = []
    for corner in range(8):
        weight = jnp.ones_like(fractions[:, 0, :])
        for dimension in range(3):
            if corner >> dimension & 1:
                weight = weight * fractions[:, dimension, :]
            else:
                weight = weight * (1.0 - fractions[:, dimension, :])
        columns.append(weight)
    return jnp.stack(columns, axis=1)


def corner_spread(weights, corners, block_rows):
    entry = jnp.arange(block_rows, dtype=jnp.int32)
    total = jnp.zeros(weights[:, 0].shape + (block_rows,), jnp.float32)
    for corner in range(8):
        hit = corners[:, corner, :, :, None] == entry
        total = total + jnp.where(hit, weights[:, corner, :, :, None], 0.0)
    return total


def candidate_onehot(slots, ray_size, slot_count, candidates):
    local_slot = slots // slot_count // ray_size * slot_count + slots % slot_count
    return (local_slot[..., None] == jnp.arange(candidates, dtype=jnp.int32)).astype(jnp.float32)


def block_partials(onehot, cot, spread):
    levels, runs, run_len, candidates = onehot.shape
    cot_rows = jnp.transpose(cot, (0, 2, 3, 1))
    scaled = onehot[:, :, :, :, None] * cot_rows[:, :, :, None, :]
    scaled = scaled.reshape(levels, runs, run_len, candidates * 4)
    return jnp.einsum("lrjc,lrje->lrce", scaled, spread, precision=lax.Precision.HIGHEST)


def on_device(
    table,
    moment1,
    moment2,
    block_ids,
    sample_slot,
    corners,
    fractions,
    feat_cot,
    weight_in,
    weight_out,
):
    table_size = lax.axis_size("table")
    ray_size = lax.axis_size("ray")
    levels, blocks_dev, features, block_rows = table.shape
    slot_count = block_ids.shape[3]
    samples = sample_slot.shape[1]
    candidates = table_size * slot_count
    run_len = samples // ray_size
    owner_here = lax.axis_index("table") * ray_size + lax.axis_index("ray")
    weights = hat_weights(fractions)
    spread = corner_spread(
        weights.reshape(levels, 8, ray_size, run_len),
        corners.reshape(levels, 8, ray_size, run_len),
        block_rows,
    )
    onehot = candidate_onehot(
        sample_slot.reshape(levels, ray_size, run_len), ray_size, slot_count, candidates
    )
    partial_value = block_partials(onehot, feat_cot.reshape(levels, 4, ray_size, run_len), spread)
    partial_value = partial_value.reshape(levels, ray_size, table_size, slot_count, 4, block_rows)
    partial_value = jnp.transpose(partial_value, (0, 2, 1, 3, 4, 5))
    routed = lax.all_to_all(partial_value, "table", split_axis=1, concat_axis=1, tiled=True)
    summed = lax.psum_scatter(routed, "ray", scatter_dimension=2, tiled=True)
    received = summed.reshape(levels, table_size * slot_count, 4 * block_rows)
    own_ids = lax.dynamic_index_in_dim(block_ids, owner_here, axis=2, keepdims=False)
    requests = jnp.transpose(own_ids, (1, 0, 2)).reshape(levels, table_size * slot_count)
    block_range = jnp.arange(blocks_dev, dtype=jnp.int32)
    selector = (requests[:, None, :] == block_range[None, :, None]).astype(jnp.float32)
    gradient = jnp.einsum("lbk,lkf->lbf", selector, received, precision=lax.Precision.HIGHEST)
    gradient = gradient.reshape(table.shape)
    first_new = beta_one * moment1 + (1.0 - beta_one) * gradient
    second_new = beta_two * moment2 + (1.0 - beta_two) * gradient * gradient
    table_new = table - learn_rate * first_new / (jnp.sqrt(second_new) + adam_eps)
    flat_table = table_new.reshape(levels, blocks_dev, 4 * block_rows)
    picked = jnp.take_along_axis(flat_table, requests[:, :, None], axis=1)
    picked = picked.reshape(levels, table_size, 1, slot_count, 4, block_rows)
    returned = lax.all_to_all(picked, "table", split_axis=1, concat_axis=1, tiled=True)
    fetched = lax.all_gather(returned, "ray", axis=2, tiled=True)
    run_tables = jnp.transpose(fetched, (0, 2, 1, 3, 4, 5)).reshape(
        levels, ray_size, candidates * 4, block_rows
    )
    looked = jnp.einsum("lrje,lrce->lrjc", spread, run_tables, precision=lax.Precision.HIGHEST)
    looked = looked.reshape(levels, ray_size, run_len, candidates, 4)
    values = jnp.sum(onehot[:, :, :, :, None] * looked, axis=3)
    encoded = jnp.transpose(values, (0, 3, 1, 2)).reshape(4 * levels, samples)
    hidden = jax.nn.relu(jnp.dot(weight_in, encoded, precision=lax.Precision.HIGHEST))
    mlp_out = jnp.dot(weight_out, hidden, precision=lax.Precision.HIGHEST)
    return (table_new, first_new, second_new, mlp_out)


def solution(mesh):
    in_specs = (
        P(None, ("table", "ray"), None, None),
        P(None, ("table", "ray"), None, None),
        P(None, ("table", "ray"), None, None),
        P(),
        P(None, ("table", "ray")),
        P(None, None, ("table", "ray")),
        P(None, None, ("table", "ray")),
        P(None, None, ("table", "ray")),
        P(),
        P(),
    )
    out_specs = (
        P(None, ("table", "ray"), None, None),
        P(None, ("table", "ray"), None, None),
        P(None, ("table", "ray"), None, None),
        P(None, ("table", "ray")),
    )
    return jax.shard_map(
        on_device, mesh=mesh, in_specs=in_specs, out_specs=out_specs, check_vma=False
    )
```

profile of v0, /device:TPU:1, one launch (start us, length us, event | category | flops | bytes accessed | tf_op | source)
XLA Modules:
  0.0 376.9 jit_solution(16789116876656948793)
XLA Ops:
  7.2 0.0 copy-start
  7.2 0.0 reduce-scatter.4.cloned.1.call-start
  7.2 0.7 fusion.14
  8.0 0.7 fusion.16
  8.7 0.1 broadcast_in_dim.97
  8.8 0.1 broadcast_in_dim.101
  8.8 0.8 reshape.206
  9.7 0.1 broadcast_in_dim.92
  9.7 0.1 broadcast_in_dim.103
  9.8 0.1 broadcast_in_dim.105
  9.9 0.1 broadcast_in_dim.107
  10.0 0.1 broadcast_in_dim.99
  10.0 0.1 broadcast_in_dim.95
  10.1 0.8 reshape.207
  10.9 0.8 reshape.208
  11.9 0.3 broadcast_multiply_fusion
  12.1 11.2 %fusion = f32[2,16,128,512]{3,2,1,0:T(8,128)} fusion(f32[2,16,32,128]{2,1,3,0:T(8,128)S(1)} %bitcast.64, f32[2,16,32]{2,1,0:T(8,128)S(1)} %broadcast_in_dim.107, s32[2,16,32]{2,1,0:T(8,128)S(1)} %get-tuple-element.8, f32[2,16,32]{2,1,0:T(8,128)S(1)} %broadcast_in_dim.105, s32[2,16,32]{2,1,0:T(8,128)S(1)} %get-tuple-element.9, ...), kind=kOutput, calls=%fused_computation.2 | convolution fusion | flops 817364992 | bytes 8978432 | tf_op jit(solution)/shard_map/lrjc,lrje->lrce/dot_general | solution.py:44
  23.4 9.8 %reshape.209 = f32[2,16,8,4,4,512]{5,4,3,2,1,0:T(4,128)} reshape(f32[2,16,128,512]{3,2,1,0:T(8,128)} %fusion) | data formatting | bytes 16777216 | tf_op jit(solution)/shard_map/reshape | solution.py:77
  33.1 10.3 %copy.52 = f32[2,16,8,4,4,512]{5,4,3,1,0,2:T(4,128)} copy(f32[2,16,8,4,4,512]{5,4,3,2,1,0:T(4,128)} %reshape.209) | data formatting | bytes 16777216 | tf_op jit(solution)/shard_map/reshape | solution.py:77
  43.5 99.5 %all_to_all.10 = f32[2,8,16,4,4,512]{5,4,3,2,0,1:T(4,128)S(1)} all-to-all(f32[2,8,16,4,4,512]{5,4,3,2,0,1:T(4,128)} %bitcast.61), channel_id=1, replica_groups=mesh['table'=8,'ray'=16] {'table'}, dimensions={1} | all-to-all | bytes 16777216 | tf_op jit(solution)/shard_map/all_to_all | solution.py:79
  143.0 10.9 %copy.41 = f32[2,8,16,4,4,512]{5,1,4,3,0,2:T(8,128)} copy(f32[2,8,16,4,4,512]{5,4,3,2,0,1:T(4,128)S(1)} %all_to_all.10) | data formatting | bytes 16777216 | tf_op jit(solution)/shard_map/all_to_all | solution.py:79
  153.9 0.0 reduce-scatter.4.cloned.1.call-update
  154.0 0.3 all-gather.2.cloned.1.call-start
  154.2 0.0 copy-done
  154.2 0.1 constant_dynamic-slice_fusion
  154.3 0.1 copy.37
  154.5 0.1 copy.38
  154.5 0.1 broadcast_in_dim_reshape.4
  154.6 0.1 eq.154
  154.7 0.1 copy.43
  154.9 0.1 reshape.216
  154.9 85.0 %reduce-scatter.4.cloned.1.call-done = f32[2,8,1,4,4,512]{5,1,4,3,0,2:T(8,128)} async-done(((f32[2,8,16,4,4,512]{5,1,4,3,0,2:T(8,128)}), f32[2,8,1,4,4,512]{5,1,4,3,0,2:T(8,128)}) %reduce-scatter.4.cloned.1.call-update) | async-done | bytes 524304
  240.0 1.4 copy.42
  241.4 0.4 reshape.210
  241.7 0.7 fusion.5
  242.4 0.7 reshape.211
  243.1 4.5 %divide_subtract_fusion = (f32[2,64,4,512]{3,2,1,0:T(4,128)S(1)}, f32[2,64,4,512]{3,2,1,0:T(4,128)}, f32[2,64,4,512]{3,2,1,0:T(4,128)}) fusion(f32[2,64,4,512]{3,2,1,0:T(4,128)} %param.10, f32[2,64,4,512]{3,2,1,0:T(4,128)S(1)} %reshape.211, f32[2,64,4,512]{3,2,1,0:T(4,128)} %param.11, f32[2,64,4,512]{3,2,1,0:T(4,128)} %param.12), kind=kLoop, calls=%fused_computation.18 | loop fusion | flops 2883584 | bytes 7340032 | tf_op jit(solution)/shard_map/sub | solution.py:90
  247.7 0.0 copy-start.2
  247.7 0.7 reshape.212
  248.4 1.2 gather_fusion
  249.6 0.0 copy-done.2
  249.6 0.4 gather.7
  250.0 0.2 copy_select_fusion
  250.2 15.6 %all_to_all.11 = f32[2,8,1,4,4,512]{5,4,3,2,0,1:T(4,128)} all-to-all(f32[2,8,1,4,4,512]{5,4,3,2,0,1:T(4,128)S(1)} %copy_select_fusion), channel_id=1, replica_groups=mesh['table'=8,'ray'=16] {'table'}, dimensions={1} | all-to-all | bytes 1048576 | tf_op jit(solution)/shard_map/all_to_all | solution.py:94
  265.8 0.0 all-gather.2.cloned.1.call-update
  265.8 68.7 %all-gather.2.cloned.1.call-done = f32[2,8,16,4,4,512]{5,4,3,2,0,1:T(4,128)} async-done(((f32[2,8,1,4,4,512]{5,4,3,2,0,1:T(4,128)}), f32[2,8,16,4,4,512]{5,4,3,2,0,1:T(4,128)}) %all-gather.2.cloned.1.call-update) | async-done | bytes 8388624 | tf_op jit(solution)/shard_map/all_gather | solution.py:95
  334.5 10.3 %copy.46 = f32[2,16,8,4,4,512]{5,4,3,2,1,0:T(4,128)} copy(f32[2,16,8,4,4,512]{5,4,3,1,0,2:T(4,128)} %bitcast.63) | data formatting | bytes 16777216 | tf_op jit(solution)/shard_map/transpose | solution.py:96
  344.9 10.0 %reshape.213 = f32[2,16,128,512]{3,2,1,0:T(8,128)} reshape(f32[2,16,8,4,4,512]{5,4,3,2,1,0:T(4,128)} %copy.46) | data formatting | bytes 16777216 | tf_op jit(solution)/shard_map/reshape | solution.py:96
  354.9 12.6 %fusion.3 = f32[2,16,32,128]{3,2,1,0:T(8,128)S(1)} fusion(f32[2,16,128,512]{3,2,1,0:T(8,128)} %reshape.213, f32[2,16,32]{2,1,0:T(8,128)S(1)} %broadcast_in_dim.107, s32[2,16,32]{2,1,0:T(8,128)S(1)} %get-tuple-element.8, f32[2,16,32]{2,1,0:T(8,128)S(1)} %broadcast_in_dim.105, s32[2,16,32]{2,1,0:T(8,128)S(1)} %get-tuple-element.9, ...), kind=kOutput, calls=%fused_computation.21 | convolution fusion | flops 817364992 | bytes 8978432 | tf_op jit(solution)/shard_map/lrje,lrce->lrjc/dot_general | solution.py:99
  367.6 0.0 copy-start.4
  367.6 0.0 copy-start.1
  367.6 0.9 copy.47
  368.5 0.0 copy-start.3
  368.5 0.3 multiply_reduce_fusion
  368.8 0.1 reshape.215
  368.9 0.0 copy-done.4
  368.9 0.3 convolution_maximum_fusion
  369.3 0.0 copy-done.3
  369.3 0.8 convolution_bitcast_fusion
  370.1 0.0 copy-done.1
  (5 shorter events, 0.1 us)
Async XLA Ops:
  7.2 147.1 %copy-start = (s32[8,2,128,4]{2,3,1,0:T(4,128)S(1)}, s32[8,2,128,4]{2,3,1,0:T(4,128)}, u32[]{:S(2)}) copy-start(s32[8,2,128,4]{2,3,1,0:T(4,128)} %param.13) | copy-start | bytes 98308
  7.2 232.8 %reduce-scatter.4.cloned.1.call-start = ((), (), s32[]{:S(2)}) async-start(), calls=%async_computation.4 | async-start | bytes 8912896
  154.0 180.6 %all-gather.2.cloned.1.call-start = ((), (), s32[]{:S(2)}) async-start(), calls=%async_computation.3 | async-start | bytes 8912896 | tf_op jit(solution)/shard_map/all_gather | solution.py:95
  247.7 1.9 copy-start.2
  367.6 1.4 copy-start.4
  367.6 2.5 copy-start.1
  368.5 0.7 copy-start.3
Sparse Core Ops, SparseCore 0:
  154.1 85.8 reduce-scatter.3
  265.9 68.5 all-gather.1
where the time goes:
time: 378 us; the launch traced here: 377 us
  waiting for transfers between devices  154 us (41%)
  blocking collectives  115 us (30%)
  local copies, waits for them, and re-layouts  60.9 us (16%)
  matrix products  25.7 us (7%)
  between operations  14.3 us (4%)
  other arithmetic  6.83 us (2%)
    all_to_all x1, blocking collectives, on_device(): lax.all_to_all(partial_value, 'table', split_axis=1, concat_axis=1, tiled...  99.5 us
    unnamed x3, waiting for transfers between devices  85.1 us
    all_gather x1, waiting for transfers between devices, on_device(): fetched = lax.all_gather(returned, 'ray', axis=2, tiled=True)  68.7 us
    reshape x2, local copies, waits for them, and re-layouts, on_device(): partial_value.reshape(levels, ray_size, table_size, slot_count, 4, block_...  20.1 us
    all_to_all x1, blocking collectives, on_device(): lax.all_to_all(picked, 'table', split_axis=1, concat_axis=1, tiled=True)  15.6 us
    dot_general x1, matrix products, on_device(): jnp.einsum('lrje,lrce->lrjc', spread, run_tables, precision=lax.Precision...  12.6 us
    dot_general x1, matrix products, block_partials(): jnp.einsum('lrjc,lrje->lrce', scaled, spread, precision=lax.Precision.HIG...  11.2 us
    all_to_all x1, local copies, waits for them, and re-layouts, on_device(): lax.all_to_all(partial_value, 'table', split_axis=1, concat_axis=1, tiled...  10.9 us
  transfers between devices with their start and end apart: 2, of which 2 were waited for; matrix products, arithmetic and copies ran while one was open for 0% of the time, Pallas kernels for 0%

commit v1 on v0

--- a/solution.py
+++ b/solution.py
@@ -92,7 +92,9 @@
     picked = jnp.take_along_axis(flat_table, requests[:, :, None], axis=1)
     picked = picked.reshape(levels, table_size, 1, slot_count, 4, block_rows)
     returned = lax.all_to_all(picked, "table", split_axis=1, concat_axis=1, tiled=True)
-    fetched = lax.all_gather(returned, "ray", axis=2, tiled=True)
+    fetched = jnp.concatenate(
+        lax.all_to_all(jnp.stack([returned] * lax.axis_size("ray")), "ray", 0, 0), axis=2
+    )
     run_tables = jnp.transpose(fetched, (0, 2, 1, 3, 4, 5)).reshape(
         levels, ray_size, candidates * 4, block_rows
     )

time: 378 us -> 401 us (1.061)
  blocking collectives: 115 us -> 214 us
  waiting for transfers between devices: 154 us -> 85.3 us
  local copies, waits for them, and re-layouts: 60.9 us -> 52.9 us
    all_to_all x0 -> x1, blocking collectives: none -> 98.7 us  [on_device(): lax.all_to_all(jnp.stack([returned] * lax.axis_size('ray')), 'ray', 0, 0)]
    all_gather x1 -> x0, waiting for transfers between devices: 68.7 us -> none  [on_device(): fetched = lax.all_gather(returned, 'ray', axis=2, tiled=True)]
    transpose x1 -> x0, local copies, waits for them, and re-layouts: 10.3 us -> none  [on_device(): jnp.transpose(fetched, (0, 2, 1, 3, 4, 5))]
    unnamed x3 -> x2, waiting for transfers between devices: 85.1 us -> 85.3 us
  transfers between devices with their start and end apart: 2 -> 1, of which waited for: 2 -> 1; matrix products, arithmetic and copies ran while one was open for 0% -> 0% of each run, Pallas kernels for 0% -> 0%
where the time goes in v1:
time: 401 us; the launch traced here: 399 us
  blocking collectives  214 us (53%)
  waiting for transfers between devices  85.3 us (21%)
  local copies, waits for them, and re-layouts  52.9 us (13%)
  matrix products  25.6 us (6%)
  between operations  14.3 us (4%)
  other arithmetic  6.83 us (2%)
    all_to_all x1, blocking collectives, on_device(): lax.all_to_all(partial_value, 'table', split_axis=1, concat_axis=1, tiled...  99.5 us
    all_to_all x1, blocking collectives, on_device(): lax.all_to_all(jnp.stack([returned] * lax.axis_size('ray')), 'ray', 0, 0)  98.7 us
    unnamed x2, waiting for transfers between devices  85.3 us
    reshape x2, local copies, waits for them, and re-layouts, on_device(): partial_value.reshape(levels, ray_size, table_size, slot_count, 4, block_...  20.1 us
    all_to_all x1, blocking collectives, on_device(): lax.all_to_all(picked, 'table', split_axis=1, concat_axis=1, tiled=True)  15.5 us
    dot_general x1, matrix products, on_device(): jnp.einsum('lrje,lrce->lrjc', spread, run_tables, precision=lax.Precision...  12.6 us
    dot_general x1, matrix products, block_partials(): jnp.einsum('lrjc,lrje->lrce', scaled, spread, precision=lax.Precision.HIG...  11.2 us
    all_to_all x1, local copies, waits for them, and re-layouts, on_device(): lax.all_to_all(partial_value, 'table', split_axis=1, concat_axis=1, tiled...  10.9 us
  transfers between devices with their start and end apart: 1, of which 1 were waited for; matrix products, arithmetic and copies ran while one was open for 0% of the time, Pallas kernels for 0%

profile of v1, /device:TPU:1, one launch (start us, length us, event | category | flops | bytes accessed | tf_op | source)
XLA Modules:
  0.0 398.8 jit_solution(11958786808203050054)
XLA Ops:
  7.2 0.0 copy-start
  7.2 0.0 reduce-scatter.4.cloned.1.call-start
  7.2 0.7 fusion.15
  8.0 0.7 fusion.17
  8.7 0.1 broadcast_in_dim.97
  8.8 0.1 broadcast_in_dim.101
  8.8 0.8 reshape.215
  9.7 0.1 broadcast_in_dim.92
  9.7 0.1 broadcast_in_dim.103
  9.8 0.1 broadcast_in_dim.105
  9.9 0.1 broadcast_in_dim.107
  10.0 0.1 broadcast_in_dim.99
  10.0 0.1 broadcast_in_dim.95
  10.1 0.8 reshape.216
  10.9 0.8 reshape.217
  11.9 0.3 broadcast_multiply_fusion
  12.1 11.2 %fusion.2 = f32[2,16,128,512]{3,2,1,0:T(8,128)} fusion(f32[2,16,32,128]{2,1,3,0:T(8,128)S(1)} %bitcast.70, f32[2,16,32]{2,1,0:T(8,128)S(1)} %broadcast_in_dim.107, s32[2,16,32]{2,1,0:T(8,128)S(1)} %get-tuple-element.8, f32[2,16,32]{2,1,0:T(8,128)S(1)} %broadcast_in_dim.105, s32[2,16,32]{2,1,0:T(8,128)S(1)} %get-tuple-element.9, ...), kind=kOutput, calls=%fused_computation.4 | convolution fusion | flops 817364992 | bytes 8978432 | tf_op jit(solution)/shard_map/lrjc,lrje->lrce/dot_general | solution.py:44
  23.4 9.8 %reshape.218 = f32[2,16,8,4,4,512]{5,4,3,2,1,0:T(4,128)} reshape(f32[2,16,128,512]{3,2,1,0:T(8,128)} %fusion.2) | data formatting | bytes 16777216 | tf_op jit(solution)/shard_map/reshape | solution.py:77
  33.2 10.3 %copy.55 = f32[2,16,8,4,4,512]{5,4,3,1,0,2:T(4,128)} copy(f32[2,16,8,4,4,512]{5,4,3,2,1,0:T(4,128)} %reshape.218) | data formatting | bytes 16777216 | tf_op jit(solution)/shard_map/reshape | solution.py:77
  43.5 99.5 %all_to_all.18 = f32[2,8,16,4,4,512]{5,4,3,2,0,1:T(4,128)S(1)} all-to-all(f32[2,8,16,4,4,512]{5,4,3,2,0,1:T(4,128)} %bitcast.67), channel_id=1, replica_groups=mesh['table'=8,'ray'=16] {'table'}, dimensions={1} | all-to-all | bytes 16777216 | tf_op jit(solution)/shard_map/all_to_all | solution.py:79
  143.0 10.9 %copy.40 = f32[2,8,16,4,4,512]{5,1,4,3,0,2:T(8,128)} copy(f32[2,8,16,4,4,512]{5,4,3,2,0,1:T(4,128)S(1)} %all_to_all.18) | data formatting | bytes 16777216 | tf_op jit(solution)/shard_map/all_to_all | solution.py:79
  153.9 0.0 reduce-scatter.4.cloned.1.call-update
  154.0 0.0 copy-done
  154.0 0.1 constant_dynamic-slice_fusion
  154.1 0.1 copy.36
  154.2 0.1 copy.37
  154.3 0.1 broadcast_in_dim_reshape.4
  154.4 0.1 eq.154
  154.5 0.1 copy.42
  154.6 0.1 reshape.227
  154.7 85.3 %reduce-scatter.4.cloned.1.call-done = f32[2,8,1,4,4,512]{5,1,4,3,0,2:T(8,128)} async-done(((f32[2,8,16,4,4,512]{5,1,4,3,0,2:T(8,128)}), f32[2,8,1,4,4,512]{5,1,4,3,0,2:T(8,128)}) %reduce-scatter.4.cloned.1.call-update) | async-done | bytes 524304
  240.0 1.4 copy.41
  241.4 0.4 reshape.219
  241.7 0.7 fusion.6
  242.4 0.7 reshape.220
  243.1 4.5 %divide_subtract_fusion = (f32[2,64,4,512]{3,2,1,0:T(4,128)S(1)}, f32[2,64,4,512]{3,2,1,0:T(4,128)}, f32[2,64,4,512]{3,2,1,0:T(4,128)}) fusion(f32[2,64,4,512]{3,2,1,0:T(4,128)} %param.10, f32[2,64,4,512]{3,2,1,0:T(4,128)S(1)} %reshape.220, f32[2,64,4,512]{3,2,1,0:T(4,128)} %param.11, f32[2,64,4,512]{3,2,1,0:T(4,128)} %param.12), kind=kLoop, calls=%fused_computation.20 | loop fusion | flops 2883584 | bytes 7340032 | tf_op jit(solution)/shard_map/sub | solution.py:90
  247.7 0.0 copy-start.2
  247.7 0.9 reshape.221
  248.6 1.2 gather_fusion
  249.8 0.0 copy-done.2
  249.8 0.4 gather.7
  250.2 0.2 copy_select_fusion
  250.4 15.5 %all_to_all.19 = f32[2,8,1,4,4,512]{5,4,3,0,2,1:T(4,128)S(1)} all-to-all(f32[2,8,1,4,4,512]{5,4,3,0,2,1:T(4,128)S(1)} %copy_select_fusion), channel_id=1, replica_groups=mesh['table'=8,'ray'=16] {'table'}, dimensions={1} | all-to-all | bytes 1048576 | tf_op jit(solution)/shard_map/all_to_all | solution.py:94
  266.0 2.1 stack.2
  268.1 98.7 %all_to_all.20 = f32[16,2,8,1,4,4,512]{6,5,4,2,1,3,0:T(4,128)} all-to-all(f32[16,2,8,1,4,4,512]{6,5,4,2,1,3,0:T(4,128)S(1)} %stack.2), channel_id=1, replica_groups=mesh['table'=8,'ray'=16] {'ray'}, dimensions={0} | all-to-all | bytes 16777216 | tf_op jit(solution)/shard_map/all_to_all | solution.py:96
  366.8 10.0 %reshape.234 = f32[2,16,128,512]{3,2,0,1:T(8,128)} reshape(f32[2,16,8,4,4,512]{5,4,3,2,0,1:T(4,128)} %bitcast.68) | data formatting | bytes 16777216 | tf_op jit(solution)/shard_map/reshape | solution.py:98
  376.8 12.6 %fusion = f32[2,16,32,128]{3,2,1,0:T(8,128)S(1)} fusion(f32[2,16,128,512]{3,2,0,1:T(8,128)} %reshape.234, f32[2,16,32]{2,1,0:T(8,128)S(1)} %broadcast_in_dim.107, s32[2,16,32]{2,1,0:T(8,128)S(1)} %get-tuple-element.8, f32[2,16,32]{2,1,0:T(8,128)S(1)} %broadcast_in_dim.105, s32[2,16,32]{2,1,0:T(8,128)S(1)} %get-tuple-element.9, ...), kind=kOutput, calls=%fused_computation.1 | convolution fusion | flops 817364992 | bytes 8978432 | tf_op jit(solution)/shard_map/lrje,lrce->lrjc/dot_general | solution.py:101
  389.4 0.0 copy-start.4
  389.5 0.0 copy-start.1
  389.5 0.9 copy.47
  390.4 0.0 copy-start.3
  390.4 0.3 multiply_reduce_fusion
  390.7 0.1 reshape.226
  390.8 0.0 copy-done.4
  390.8 0.3 convolution_maximum_fusion
  391.1 0.0 copy-done.3
  391.1 0.8 convolution_bitcast_fusion
  392.0 0.0 copy-done.1
  (6 shorter events, 0.1 us)
Async XLA Ops:
  7.2 146.8 %copy-start = (s32[8,2,128,4]{2,3,1,0:T(4,128)S(1)}, s32[8,2,128,4]{2,3,1,0:T(4,128)}, u32[]{:S(2)}) copy-start(s32[8,2,128,4]{2,3,1,0:T(4,128)} %param.13) | copy-start | bytes 98308
  7.2 232.8 %reduce-scatter.4.cloned.1.call-start = ((), (), s32[]{:S(2)}) async-start(), calls=%async_computation.4 | async-start | bytes 8912896
  247.7 2.2 copy-start.2
  389.4 1.4 copy-start.4
  389.5 2.5 copy-start.1
  390.4 0.7 copy-start.3
Sparse Core Ops, SparseCore 0:
  154.1 85.8 reduce-scatter.3
